TPU v7x, 32 devices: a whole 2x2x4 slice. The times are simulated.
32 devices in a mesh: row: 4 (over y, core), col: 8 (over z, x).
Axes of the slice: x: 2, y: 2, z: 4, core: 2. Of those that a mesh axis runs over, the one named last changes fastest.
Arguments:
- a_vals: bfloat16 [256, 131072], P('row', 'col'), may hold values from -1.1953125 to 1.1953125
- p_vals: bfloat16 [64, 16384], P(None, ('row', 'col')), may hold values from -0.75 to 0.75
- a_rows: int32 [4, 2048], P('row', 'col'), may hold values from 0 to 63, as said below
- a_cols: int32 [4, 2048], P('row', 'col'), may hold values from 0 to 31, as said below
- a_count: int32 [4, 8], P('row', 'col'), may hold values from 64 to 256, as said below
- c_slot: int32 [4, 2048], P('row', 'col'), may hold values from 0 to 5, as said below
- agg: int32 [256], P(('row', 'col')), may hold values from 0 to 7, as said below
Outputs:
- coarse_vals: float32 [32, 24576], P(('row', 'col'))
Inputs may be any that keep to these rules, and one draw needn't show every extreme that they name: Each tile's live slots are its first a_count ones; some tile of every row group has all 256 slots live. `agg`: in each row group, the aggregate numbers t*32//8 to (t+1)*32//8 - 1 are taken by the fine block rows of the row group's t-th column group of 32 rows, each number by exactly 8 of them. Coarse pattern: in row group r, slot k of coarse row a belongs to column group (a*6 + k + o_r) mod 8, for one shift o_r of the row group, and to one aggregate of that column group; every tile slot, live or not, has a fine row of aggregate a and a fine column of that slot's aggregate, with c_slot = k. The live slots of each tile reach every (a, k) pair of its column group. `a_rows`: see c_slot. `a_cols`: see c_slot.
All inputs are finite; a program needn't handle non-finite values.
Results may differ from a plain program's by a relative error of at most 0.0049.
Values may be sent and summed in bfloat16 or wider, within the bound.
A program may use at most 64 MiB of HBM per device.

v0:
```python
import functools

import jax
import jax.numpy as jnp
from jax import lax
from jax.experimental import pallas as pl
from jax.experimental.pallas import tpu as pltpu
from jax.sharding import PartitionSpec as P

AGG = 8
KC = 6
LO = 2
UNROLL = 32
MESH = pl.DeviceIdType.MESH
F32 = jnp.float32
BF16 = jnp.bfloat16


def within(at, size):
    return jnp.minimum(jnp.maximum(at, 0), size - 1)


def make_plan(rows_group, cols_group, dev_rows, small, count_v, plan_v):
    slots, width = small.shape[2], plan_v.shape[1]
    cb, sb, db = (n.bit_length() - 1 for n in (cols_group, slots, dev_rows))
    rows, cols = small[0], small[1]
    lane = lax.broadcasted_iota(jnp.int32, (1, slots), 1)
    key = jnp.where(lane < count_v[...], rows, rows_group)
    across = jnp.broadcast_to(((((key << sb) | lane) << cb) | cols), (slots, slots))
    side = lax.broadcasted_iota(jnp.int32, (slots, slots), 0)
    place = lax.broadcasted_iota(jnp.int32, (slots, slots), 1)
    down = jnp.sum(jnp.where(side == place, across, 0), axis=1, keepdims=True)
    rank = jnp.sum(jnp.where(across < down, 1, 0), axis=1, keepdims=True)
    word = jnp.sum(jnp.where(rank == place, down, 0), axis=0, keepdims=True)
    slot = (word >> cb) & (slots - 1)
    top = word >> (cb + sb)
    same = (top == pltpu.roll(top, 1, 1)) & (lane > 0)
    target = lax.broadcasted_iota(jnp.int32, (slots, width), 1)
    tops = down >> (cb + sb)
    upto = jnp.sum(jnp.where(tops <= target, 1, 0), axis=0, keepdims=True)
    before = jnp.sum(jnp.where(tops < target, 1, 0), axis=0, keepdims=True)
    last = jnp.where(upto > before, upto - 1, slots)
    plan_v[...] = jnp.zeros_like(plan_v)
    right = 2 * (word & (cols_group - 1)) + (slot & 1)
    plan_v[0:1, :slots] = (slot >> 1) | (same.astype(jnp.int32) << 15) | (right << 16)
    plan_v[3:4, :] = last
    plan_v[4:5, :slots] = rows >> db
    plan_v[5:6, :slots] = rows & (dev_rows - 1)
    plan_v[6:7, :slots] = small[2]


def kernel(
    n_row, n_col, a_hbm, p_hbm, rows_hbm, cols_hbm, count_hbm, kslot_hbm, agg_hbm, out_ref,
    small, count_v, agg_v, plan_v, plan_s, ag_ref, in_sem, plan_sem, a_v, pan, agp, colp, pz, ps, q_ref, snd, rcv,
    a_sem, p_send, p_recv, g_send, g_recv, c_send, c_recv, x_send, x_recv,
):
    bw = p_hbm.shape[0]
    dev_rows = ag_ref.shape[0]
    rows_group = n_col * dev_rows
    slots = ps.shape[0] - 1
    ratio = n_col // n_row
    per = n_col // ratio
    owners = per * dev_rows // AGG
    hi = n_col // LO
    row = lax.axis_index("row")
    me = lax.axis_index("col")
    z, x = me // LO, lax.rem(me, LO)
    is_root = row == me // ratio
    part = lax.rem(me, ratio)

    def col_of(d):
        return lax.rem(me + d, n_col)

    barrier = pltpu.get_barrier_semaphore()
    for d in range(1, n_col):
        pl.semaphore_signal(barrier, inc=1, device_id=(row, col_of(d)), device_id_type=MESH)
    for d in range(1, n_row):
        pl.semaphore_signal(
            barrier, inc=1, device_id=(lax.rem(row + d, n_row), me), device_id_type=MESH
        )
    p_ref = pan.at[me]
    loads = [
        pltpu.make_async_copy(src, dst, in_sem.at[i])
        for i, (src, dst) in enumerate(
            [
                (p_hbm, p_ref),
                (rows_hbm, small.at[0]),
                (cols_hbm, small.at[1]),
                (kslot_hbm, small.at[2]),
                (count_hbm, count_v),
                (agg_hbm, agg_v),
            ]
        )
    ]
    for c in loads:
        c.start()

    for c in loads:
        c.wait()
    square = (dev_rows, dev_rows)
    eye = lax.broadcasted_iota(jnp.int32, square, 0) == lax.broadcasted_iota(jnp.int32, square, 1)
    mine = jnp.where(eye, jnp.broadcast_to(agg_v[...].astype(F32), square), 0.0)
    mine = jnp.broadcast_to(jnp.sum(mine, axis=1, keepdims=True), ag_ref.shape)
    ag_ref[...] = mine
    agp[me] = mine
    make_plan(rows_group, n_col // (n_col // n_row) * dev_rows, dev_rows, small, count_v, plan_v)
    pl.semaphore_wait(barrier, n_col + n_row - 2)

    def remote(src, dst, s, r, dev):
        return pltpu.make_async_remote_copy(
            src_ref=src, dst_ref=dst, send_sem=s, recv_sem=r, device_id=dev, device_id_type=MESH
        )

    own = []
    for d in range(1, hi):
        to = lax.rem(z + d, hi) * LO + x
        own.append(remote(p_ref, pan.at[me], p_send.at[len(own)], p_recv.at[me], (row, to)))
    partner = z * LO + (1 - x)
    own.append(remote(p_ref, pan.at[me], p_send.at[len(own)], p_recv.at[me], (row, partner)))
    for c in own:
        c.start()

    def panel_copies(q, src):
        m = lax.rem(q, per)
        return [
            remote(
                src, colp.at[m], c_send.at[m, d - 1], c_recv.at[m],
                (lax.rem(row + d, n_row), me),
            )
            for d in range(1, n_row)
        ]

    def hand_on(q, src):
        @pl.when(is_root & (q // per == part))
        def _():
            for c in panel_copies(q, src):
                c.start()

    plan_copy = pltpu.make_async_copy(plan_v, plan_s, plan_sem)
    plan_copy.start()
    hand_on(me, p_ref)
    marks = [
        remote(ag_ref, agp.at[me], g_send.at[d - 1], g_recv.at[me], (row, col_of(d)))
        for d in range(1, n_col)
    ]
    for c in marks:
        c.start()

    @pl.loop(0, slots // 16)
    def _(g):
        for u in range(8):
            i = g * 8 + u
            lanes = pl.ds(pl.multiple_of(i * (2 * bw), 2 * bw), 2 * bw)
            pltpu.make_async_copy(a_hbm.at[:, lanes], a_v.at[i], a_sem).start()

    pz[...] = jnp.zeros_like(pz)
    ps[slots] = jnp.zeros((bw, bw), BF16)
    q_ref[...] = jnp.zeros_like(q_ref)

    def landed(q):
        remote(p_ref, pan.at[q], p_send.at[0], p_recv.at[q], (row, partner)).wait_recv()

    passed = []
    landed(partner)
    hand_on(partner, pan.at[partner])
    for d in range(1, hi):
        q = lax.rem(z + hi - d, hi) * LO + x
        landed(q)
        c = remote(
            pan.at[q], pan.at[q], p_send.at[hi - 1 + d], p_recv.at[q], (row, partner)
        )
        c.start()
        passed.append(c)
        hand_on(q, pan.at[q])
    for d in range(1, hi):
        q = lax.rem(z + hi - d, hi) * LO + (1 - x)
        landed(q)
        hand_on(q, pan.at[q])

    for m in range(per):
        @pl.when(is_root)
        def _():
            colp[m] = pan[part * per + m]

        @pl.when(jnp.logical_not(is_root))
        def _():
            remote(
                p_ref, colp.at[m], c_send.at[m, 0], c_recv.at[m], (row, partner)
            ).wait_recv()

        for b in range(dev_rows):
            block = colp[m, :, b * bw:(b + 1) * bw]
            pz[2 * (m * dev_rows + b), 0:bw, :] = block
            pz[2 * (m * dev_rows + b) + 1, bw:2 * bw, :] = block
    pltpu.make_async_copy(a_v, a_v, a_sem).wait()

    plan_copy.wait()

    def steps(it, acc):
        for u in range(UNROLL):
            at = it * UNROLL + u
            word = plan_s[0, at]
            left = a_v[word & (slots // 2 - 1)]
            right = pz[(word >> 16) & (pz.shape[0] - 1)]
            keep = ((word >> 15) & 1).astype(F32)
            prod = jnp.dot(left, right, preferred_element_type=F32)
            acc = acc * keep + prod
            ps[at] = acc.astype(BF16)
        return acc

    lax.fori_loop(0, slots // UNROLL, steps, jnp.zeros((bw, bw), F32))

    for d in range(1, n_col):
        q = col_of(d)
        remote(ag_ref, agp.at[q], g_send.at[0], g_recv.at[q], (row, partner)).wait_recv()

    lane = lax.broadcasted_iota(jnp.int32, (1, 2 * bw), 1)

    def fold(c):
        group = c // per
        base = (group * owners).astype(F32)
        total = jnp.zeros((owners * bw, bw), F32)
        for h in range(dev_rows // 4):
            wide = []
            for e in range(2):
                b = 4 * h + 2 * e
                flip = pan[c, :, b * bw:(b + 2) * bw].T
                pair = jnp.concatenate([flip[:bw], flip[bw:]], axis=1)
                mark = jnp.where(lane < bw, agp[c, b:b + 1, :], agp[c, b + 1:b + 2, :]) - base
                wide.append(
                    jnp.concatenate(
                        [pair * jnp.where(mark == o, 1.0, 0.0).astype(BF16) for o in range(owners)],
                        axis=0,
                    )
                )
            right = jnp.concatenate(
                [ps[within(plan_s[3, c * dev_rows + 4 * h + e], slots + 1)] for e in range(4)], axis=0
            )
            total += jnp.dot(
                jnp.concatenate(wide, axis=1), right, preferred_element_type=F32
            )
        return total

    def fold_two(i, carry):
        q_ref[2 * i // per] += fold(2 * i) + fold(2 * i + 1)
        return carry

    half = bw // 2

    def term(o):
        return remote(snd.at[o], rcv.at[me], x_send.at[o], x_recv.at[me], (row, o))

    for g in range(ratio):
        lax.fori_loop(g * per // 2, (g + 1) * per // 2, fold_two, 0)
        for w in range(owners):
            o = g * owners + w
            even = q_ref[g, pl.ds(w * bw, half, stride=2), :]
            odd = q_ref[g, pl.ds(w * bw + 1, half, stride=2), :]
            snd[o] = jnp.concatenate([even, odd], axis=1).astype(BF16)
        for w in range(owners):
            o = g * owners + w

            @pl.when(me != o)
            def _():
                term(o).start()

    rcv[me] = snd[me]

    there = lax.broadcasted_iota(jnp.int32, (dev_rows, 2 * bw), 0) == plan_s[5, 0]
    spot = jnp.sum(jnp.where(there, agp[within(plan_s[4, 0], n_col)], 0.0), axis=0, keepdims=True)
    spot = spot.astype(jnp.int32) * KC + plan_s[6, 0]
    for d in range(1, n_col):
        q = col_of(d)
        remote(snd.at[0], rcv.at[q], x_send.at[0], x_recv.at[q], (row, partner)).wait_recv()
    sums = [jnp.zeros((half, 2 * bw), F32) for _ in range(KC)]
    for c in range(n_col):
        value = rcv[c].astype(F32)
        where = (spot + (c - (KC + 1) * me + 8 * n_col * n_col)) & (n_col - 1)
        for k in range(KC):
            sums[k] += jnp.where(where == k, value, 0.0)
    for k in range(KC):
        out_ref[k * half:(k + 1) * half, :] = sums[k].astype(BF16)

    for c in own + passed + marks:
        c.wait_send()
    for o in range(n_col):
        @pl.when(me != o)
        def _():
            term(o).wait_send()

    for m in range(per):
        @pl.when(is_root)
        def _():
            for c in panel_copies(m, pan.at[0]):
                c.wait_send()


def on_device(n_row, n_col, a_vals, p_vals, a_rows, a_cols, a_count, c_slot, agg):
    bw = p_vals.shape[0]
    dev_rows = agg.shape[0]
    slots = a_rows.shape[1]
    rows_group = dev_rows * n_col
    ratio = n_col // n_row
    cols_group = rows_group // ratio
    per = n_col // ratio
    assert rows_group // AGG == n_col and n_col >= KC
    assert all(n & (n - 1) == 0 for n in (n_col, slots, cols_group, dev_rows))
    keep = pl.BlockSpec(memory_space=pltpu.HBM)
    vmem = pl.BlockSpec(memory_space=pltpu.VMEM)
    dma = pltpu.SemaphoreType.DMA
    owners = per * dev_rows // AGG
    out = pl.pallas_call(
        functools.partial(kernel, n_row, n_col),
        out_shape=jax.ShapeDtypeStruct((KC * bw // 2, 2 * bw), BF16),
        in_specs=[keep] * 7,
        out_specs=vmem,
        scratch_shapes=[
            pltpu.VMEM((3, 1, slots), jnp.int32),
            pltpu.VMEM((1, 1), jnp.int32),
            pltpu.VMEM((1, dev_rows), jnp.int32),
            pltpu.VMEM((8, max(slots, rows_group)), jnp.int32),
            pltpu.SMEM((8, max(slots, rows_group)), jnp.int32),
            pltpu.VMEM((dev_rows, 2 * bw), F32),
            dma((6,)), dma,
            pltpu.VMEM((slots // 2, bw, 2 * bw), BF16),
            pltpu.VMEM((n_col, bw, dev_rows * bw), BF16),
            pltpu.VMEM((n_col, dev_rows, 2 * bw), F32),
            pltpu.VMEM((per, bw, dev_rows * bw), BF16),
            pltpu.VMEM((2 * cols_group, 2 * bw, bw), BF16),
            pltpu.VMEM((slots + 1, bw, bw), BF16),
            pltpu.VMEM((ratio, owners * bw, bw), F32),
            pltpu.VMEM((n_col, bw // 2, 2 * bw), BF16),
            pltpu.VMEM((n_col, bw // 2, 2 * bw), BF16),
            dma,
            dma((n_col,)), dma((n_col,)),
            dma((n_col,)), dma((n_col,)),
            dma((per, n_row)), dma((per,)),
            dma((n_col,)), dma((n_col,)),
        ],
        compiler_params=pltpu.CompilerParams(
            collective_id=0, has_side_effects=True, vmem_limit_bytes=67043328
        ),
    )(a_vals, p_vals, a_rows, a_cols, a_count, c_slot, agg.reshape(1, dev_rows))
    return out.astype(F32).reshape(1, KC * bw * bw)


def solution(mesh):
    return jax.shard_map(
        functools.partial(on_device, mesh.shape["row"], mesh.shape["col"]),
        mesh=mesh,
        in_specs=(
            P("row", "col"),
            P(None, ("row", "col")),
            P("row", "col"),
            P("row", "col"),
            P("row", "col"),
            P("row", "col"),
            P(("row", "col")),
        ),
        out_specs=P(("row", "col"), None),
        check_vma=False,
    )
```

profile of v0, /device:TPU:0, one launch (start us, length us, event | category | flops | bytes accessed | tf_op | source)
XLA Modules:
  0.0 31.2 jit_solution(6496667888612302217)
XLA Ops:
  0.7 29.0 %shard_map.73 = bf16[192,128]{1,0:T(8,128)(2,1)} custom-call(bf16[64,16384]{1,0:T(8,128)(2,1)} %a_hbm.1, bf16[64,512]{1,0:T(8,128)(2,1)} %p_hbm.1, s32[1,256]{1,0:T(1,128)} %rows_hbm.1, s32[1,256]{1,0:T(1,128)} %cols_hbm.1, s32[1,1]{1,0:T(1,128)S(6)} %copy.8.count_hbm, s32[1,256]{1,0:T(1,128)} %kslot_hbm.1, s32[1,8]{1,0:T(1,128)} %bitcast.2), custom_call_target="tpu_custom_call" | custom-call | tf_op jit(solution)/shard_map/pallas_call | solution.py:312
  29.7 1.4 %reshape.12 = f32[192,128]{1,0:T(8,128)} convert(bf16[192,128]{1,0:T(8,128)(2,1)} %shard_map.73) | non-fusion elementwise | flops 24576 | bytes 147456 | tf_op jit(solution)/shard_map/reshape | solution.py:344
where the time goes:
time: 31.4 us; the launch traced here: 31.2 us
  Pallas kernels  29 us (92%)
  other arithmetic  1.45 us (5%)
  between operations  0.66 us (2%)
    pallas_call x1, Pallas kernels, on_device(): pl.pallas_call(functools.partial(kernel, n_row, n_col), out_shape=jax.Sha...  29 us
    reshape x1, other arithmetic, on_device(): return out.astype(F32).reshape(1, KC * bw * bw)  1.45 us

commit v1 on v0

v1 whole, which is shorter than its diff:
```python
import functools

import jax
import jax.numpy as jnp
from jax import lax
from jax.experimental import pallas as pl
from jax.experimental.pallas import tpu as pltpu
from jax.sharding import PartitionSpec as P

AGG = 8
KC = 6
LO = 2
MESH = pl.DeviceIdType.MESH
F32 = jnp.float32
BF16 = jnp.bfloat16
I32 = jnp.int32


def iota(shape, dim):
    return lax.broadcasted_iota(I32, shape, dim)


def within(at, size):
    return jnp.minimum(jnp.maximum(at, 0), size - 1)


def bits(n):
    return n.bit_length() - 1


def sort_slots(rows_group, cols_group, small, count_v, plan_v, down_v, tag_v):
    slots = small.shape[2]
    cb, sb = bits(cols_group), bits(slots)
    rows, cols = small[0], small[1]
    lane = iota((1, slots), 1)
    key = jnp.where(lane < count_v[...], rows, rows_group)
    across = jnp.broadcast_to(((((key << cb) | cols) << sb) | lane), (slots, slots))
    side, place = iota((slots, slots), 0), iota((slots, slots), 1)
    down = jnp.sum(jnp.where(side == place, across, 0), axis=1, keepdims=True)
    rank = jnp.sum(jnp.where(across < down, 1, 0), axis=1, keepdims=True)
    more = jnp.where((across >> sb == down >> sb) & (across > down), 1, 0)
    more = jnp.sum(more, axis=1, keepdims=True)
    word = jnp.sum(jnp.where(rank == place, down, 0), axis=0, keepdims=True)
    slot, top = word & (slots - 1), word >> sb
    same = (top == pltpu.roll(top, 1, 1)) & (lane > 0)
    plan_v[0:1, :slots] = slot | (same.astype(I32) << 15)
    last = (more == 0) & (down >> (cb + sb) < rows_group)
    down_v[...] = jnp.broadcast_to(down >> sb, down_v.shape)
    tag_v[...] = jnp.broadcast_to(jnp.where(last, rank + 1, 0), tag_v.shape)


def ranks(marks, width):
    n = marks.shape[0]
    side, place = iota((n, width), 0), iota((n, width), 1)
    down = jnp.broadcast_to(marks[:, 0:1], (n, width))
    across = jnp.sum(jnp.where(side == place, down, 0), axis=0, keepdims=True)
    across = jnp.where(place[0:1] < n, across, -1)
    alike = down == across
    along = jnp.sum(jnp.where(alike & (side < place), 1, 0), axis=0, keepdims=True)
    below = jnp.sum(jnp.where(alike & (place < side), 1, 0), axis=1, keepdims=True)
    return across, along, below


def make_tables(rows_group, cols_group, slots, row_marks, col_marks, down_v, tag_v, plan_v):
    cb = bits(cols_group)
    width, wide = max(rows_group, 128), max(cols_group, 128)
    agg, place, below = ranks(row_marks, width)
    target, spot, under = ranks(col_marks, wide)
    pair = agg * AGG + place
    down = down_v[:, 0:1]
    tag = tag_v[:, 0:1]
    row, col = down >> cb, down & (cols_group - 1)
    at_row = row == iota((slots, width), 1)
    at_col = col == iota((slots, wide), 1)
    left = jnp.sum(jnp.where(at_row, pair, 0), axis=1, keepdims=True)
    right = jnp.sum(jnp.where(at_col, target * AGG + spot, 0), axis=1, keepdims=True)
    cell = left * AGG + (right & (AGG - 1))
    cells = rows_group * AGG
    step = min(cells, 512)
    for g in range(cells // step):
        q = iota((slots, step), 1) + g * step
        found = jnp.sum(jnp.where(cell == q, tag, 0), axis=0, keepdims=True)
        plan_v[1:2, g * step:(g + 1) * step] = jnp.where(found > 0, found - 1, slots)
    q = iota((rows_group, width), 1)
    mine = row_marks[:, 0:1] * AGG + below
    listed = jnp.sum(jnp.where(mine == q, iota((rows_group, width), 0), 0), axis=0, keepdims=True)
    plan_v[2:3, :width] = listed
    q = iota((slots, width), 1)
    live = (row < rows_group) & (left >> bits(AGG) == q >> bits(AGG))
    aim = jnp.max(jnp.where(live, right >> bits(AGG), -1), axis=0, keepdims=True)
    q = iota((cols_group, width), 1)
    hit = (col_marks[:, 0:1] == aim) & (under == (q & (AGG - 1)))
    listed = jnp.sum(jnp.where(hit, iota((cols_group, width), 0), 0), axis=0, keepdims=True)
    plan_v[3:4, :width] = listed


def kernel(
    n_row, n_col, a_hbm, p_hbm, rows_hbm, cols_hbm, count_hbm, kslot_hbm, agg_hbm, out_ref,
    small, count_v, agg_v, plan_v, plan_s, down_v, tag_v, agp, cgp, a_v, side, summed,
    pan, colp, flip, colb, terms, snd, rcv,
    in_sem, a_sem, plan_sem, p_send, p_recv, g_send, g_recv, c_send, c_recv, m_send, m_recv, x_send, x_recv,
):
    bw = p_hbm.shape[0]
    dev_rows = agg_v.shape[1]
    rows_group = n_col * dev_rows
    slots = small.shape[2]
    ratio = n_col // n_row
    per = n_col // ratio
    cols_group = per * dev_rows
    hi = n_col // LO
    half = bw // 2
    row = lax.axis_index("row")
    me = lax.axis_index("col")
    z, x = me // LO, lax.rem(me, LO)
    partner = z * LO + (1 - x)
    root = me // ratio
    part = lax.rem(me, ratio)
    is_root = row == root
    alike = lax.rem(row, 2) == lax.rem(root, 2)
    is_head = alike & jnp.logical_not(is_root)
    twin_row = row + 1 - 2 * lax.rem(row, 2)

    def col_of(d):
        return lax.rem(me + d, n_col)

    def row_of(d):
        return lax.rem(row + d, n_row)

    def z_of(d):
        return jnp.bitwise_xor(z, d)

    barrier = pltpu.get_barrier_semaphore()
    for d in range(1, n_col):
        pl.semaphore_signal(barrier, inc=1, device_id=(row, col_of(d)), device_id_type=MESH)
    for d in range(1, n_row):
        pl.semaphore_signal(barrier, inc=1, device_id=(row_of(d), me), device_id_type=MESH)
    loads = [
        pltpu.make_async_copy(src, dst, in_sem.at[i])
        for i, (src, dst) in enumerate(
            [
                (agg_hbm, agg_v),
                (rows_hbm, small.at[0]),
                (cols_hbm, small.at[1]),
                (count_hbm, count_v),
                (kslot_hbm, small.at[2]),
                (p_hbm, pan.at[me]),
            ]
        )
    ]
    for c in loads:
        c.start()
    pl.semaphore_wait(barrier, n_col + n_row - 2)

    def remote(src, dst, s, r, dev):
        return pltpu.make_async_remote_copy(
            src_ref=src, dst_ref=dst, send_sem=s, recv_sem=r, device_id=dev, device_id_type=MESH
        )

    own = [remote(p_hbm, pan.at[me], p_send.at[0], p_recv.at[me], (row, partner))]
    for d in range(1, hi):
        own.append(
            remote(p_hbm, pan.at[me], p_send.at[d], p_recv.at[me], (row, z_of(d) * LO + x))
        )
    for c in own:
        c.start()

    def panel_copies(q, src):
        m = lax.rem(q, per)
        copies = [remote(src, colp.at[m], c_send.at[m, 0], c_recv.at[m], (twin_row, me))]
        for d in range(1, n_row // 2):
            copies.append(
                remote(src, colp.at[m], c_send.at[m, d], c_recv.at[m], (row_of(2 * d), me))
            )
        return copies

    def hand_on(q, src):
        @pl.when(is_root & (q // per == part))
        def _():
            for c in reversed(panel_copies(q, src)):
                c.start()

    hand_on(me, p_hbm)

    @pl.loop(0, slots // 16)
    def _(g):
        for u in range(8):
            i = g * 8 + u
            lanes = pl.ds(pl.multiple_of(i * (2 * bw), 2 * bw), 2 * bw)
            pltpu.make_async_copy(a_hbm.at[:, lanes], a_v.at[i], a_sem).start()

    loads[0].wait()
    square = (dev_rows, dev_rows)
    eye = iota(square, 0) == iota(square, 1)
    mine = jnp.where(eye, jnp.broadcast_to(agg_v[...], square), 0)
    mine = jnp.sum(mine, axis=1, keepdims=True)
    agp[me] = jnp.broadcast_to(mine, agp.shape[1:])
    marks = [
        remote(agp.at[me], agp.at[me], g_send.at[d - 1], g_recv.at[me], (row, col_of(d)))
        for d in range(1, n_col)
    ]
    for c in marks:
        c.start()
    for c in loads[1:]:
        c.wait()
    sort_slots(rows_group, cols_group, small, count_v, plan_v, down_v, tag_v)
    plan_copy = pltpu.make_async_copy(plan_v, plan_s, plan_sem)
    plan_copy.start()
    lanes = iota((bw, 2 * bw), 1)
    side[0] = (lanes < bw).astype(F32).astype(BF16)
    side[1] = (lanes >= bw).astype(F32).astype(BF16)
    summed[slots] = jnp.zeros((bw, 2 * bw), BF16)

    def landed(q):
        remote(p_hbm, pan.at[q], p_send.at[0], p_recv.at[q], (row, partner)).wait_recv()

    def turn(q):
        for h in range(dev_rows // 2):
            t = pan[q, :, 2 * h * bw:2 * (h + 1) * bw].T
            for e in range(2):
                block = t[e * bw:(e + 1) * bw]
                flip[q * dev_rows + 2 * h + e] = jnp.concatenate([block, block], axis=1)

    pltpu.make_async_copy(a_v, a_v, a_sem).wait()

    plan_copy.wait()

    def sums(lo, hi_, acc):
        def body(i, acc):
            for u in range(8):
                word = plan_s[0, 8 * i + u]
                keep = ((word >> 15) & 1).astype(F32)
                pair = a_v[(word & (slots - 1)) >> 1] * side[word & 1]
                acc = acc * keep + pair.astype(F32)
                summed[8 * i + u] = acc.astype(BF16)
            return acc

        return lax.fori_loop(lo, hi_, body, acc)

    landed(partner)
    hand_on(partner, pan.at[partner])
    turn(me)
    turn(partner)
    acc = sums(0, slots // 16, jnp.zeros((bw, 2 * bw), F32))
    passed = []
    for d in range(1, hi):
        q = z_of(d) * LO + x
        landed(q)
        c = remote(pan.at[q], pan.at[q], p_send.at[hi - 1 + d], p_recv.at[q], (row, partner))
        c.start()
        passed.append(c)
        hand_on(q, pan.at[q])
        turn(q)
    acc = sums(slots // 16, slots // 8, acc)

    for d in range(1, n_col):
        q = col_of(d)
        remote(agp.at[q], agp.at[q], g_send.at[0], g_recv.at[q], (row, partner)).wait_recv()

    @pl.when(is_root)
    def _():
        for m in range(per):
            cgp[m] = agp[part * per + m]

    def mark_copies():
        return [
            remote(cgp, cgp, m_send.at[d - 1], m_recv, (row_of(d), me)) for d in range(1, n_row)
        ]

    @pl.when(is_root)
    def _():
        for c in mark_copies():
            c.start()

    for d in range(1, hi):
        q = z_of(d) * LO + (1 - x)
        landed(q)
        hand_on(q, pan.at[q])
        turn(q)

    @pl.when(jnp.logical_not(is_root))
    def _():
        remote(cgp, cgp, m_send.at[0], m_recv, (row, partner)).wait_recv()

    row_marks = jnp.concatenate([agp[c] for c in range(n_col)], axis=0)
    col_marks = jnp.concatenate([cgp[m] for m in range(per)], axis=0)
    make_tables(rows_group, cols_group, slots, row_marks, col_marks, down_v, tag_v, plan_v)
    there = iota((rows_group, 2 * bw), 0) == small[0, 0:1, 0:1]
    first = jnp.sum(jnp.where(there, row_marks, 0), axis=0, keepdims=True)
    first = first * KC + small[2, 0:1, 0:1]
    plan_copy.start()
    plan_copy.wait()

    in_left = (iota((bw, 2 * bw), 1) < bw).astype(F32).astype(BF16)
    in_right = (iota((bw, 2 * bw), 1) >= bw).astype(F32).astype(BF16)

    def join(left, right):
        return left * in_left + right * in_right

    def unpack(m, src):
        for b in range(dev_rows):
            colb[m * dev_rows + b] = src[:, b * bw:(b + 1) * bw]

    for m in range(per):
        @pl.when(is_root)
        def _():
            unpack(m, pan.at[part * per + m])

        @pl.when(jnp.logical_not(is_root))
        def _():
            remote(
                p_hbm, colp.at[m], c_send.at[m, 0], c_recv.at[m], (row, partner)
            ).wait_recv()

            @pl.when(is_head)
            def _():
                panel_copies(m, colp.at[m])[0].start()

            unpack(m, colp.at[m])

    aggs = rows_group // AGG
    block = min(aggs, 8)

    def fold(g, carry):
        for u in range(block):
            a = g * block + u
            right = jnp.concatenate(
                [colb[plan_s[3, a * AGG + n // 2]] for n in range(2 * AGG)], axis=0
            )
            mat = jnp.concatenate(
                [
                    jnp.concatenate(
                        [summed[plan_s[1, (a * AGG + m) * AGG + n]] for n in range(AGG)], axis=1
                    )
                    for m in range(AGG)
                ],
                axis=0,
            )
            left = jnp.concatenate(
                [
                    join(
                        flip[plan_s[2, a * AGG + 2 * h]],
                        flip[plan_s[2, a * AGG + 2 * h + 1]],
                    )
                    for h in range(AGG // 2)
                ],
                axis=1,
            )
            mid = jnp.dot(left, mat, preferred_element_type=F32).astype(BF16)
            terms[a] = jnp.dot(mid, right, preferred_element_type=F32)
        for u in range(block):
            a = g * block + u
            even = terms[a, pl.ds(0, half, stride=2), :]
            odd = terms[a, pl.ds(1, half, stride=2), :]
            snd[a] = jnp.concatenate([even, odd], axis=1).astype(BF16)
        return carry

    lax.fori_loop(0, aggs // block, fold, 0)

    def term(o):
        return remote(snd.at[o], rcv.at[me], x_send.at[o], x_recv.at[me], (row, o))

    for o in range(n_col):
        @pl.when(me != o)
        def _():
            term(o).start()

    rcv[me] = snd[me]
    for d in range(1, n_col):
        q = col_of(d)
        remote(snd.at[0], rcv.at[q], x_send.at[0], x_recv.at[q], (row, partner)).wait_recv()
    total = [jnp.zeros((half, 2 * bw), F32) for _ in range(KC)]
    for c in range(n_col):
        value = rcv[c].astype(F32)
        where = (first + (c - (KC + 1) * me + 8 * n_col * n_col)) & (n_col - 1)
        for k in range(KC):
            total[k] += jnp.where(where == k, value, 0.0)
    for k in range(KC):
        out_ref[k * half:(k + 1) * half, :] = total[k].astype(BF16)

    for c in own + passed + marks:
        c.wait_send()
    for o in range(n_col):
        @pl.when(me != o)
        def _():
            term(o).wait_send()

    @pl.when(is_root)
    def _():
        for c in mark_copies():
            c.wait_send()
        for m in range(per):
            for c in panel_copies(m, pan.at[0]):
                c.wait_send()

    @pl.when(is_head)
    def _():
        for m in range(per):
            panel_copies(m, colp.at[m])[0].wait_send()


def on_device(n_row, n_col, a_vals, p_vals, a_rows, a_cols, a_count, c_slot, agg):
    bw = p_vals.shape[0]
    dev_rows = agg.shape[0]
    slots = a_rows.shape[1]
    rows_group = dev_rows * n_col
    ratio = n_col // n_row
    per = n_col // ratio
    cols_group = per * dev_rows
    hi = n_col // LO
    assert rows_group // AGG == n_col and n_col >= KC and n_row % 2 == 0
    assert all(n & (n - 1) == 0 for n in (n_col, slots, cols_group, dev_rows, hi))
    keep = pl.BlockSpec(memory_space=pltpu.HBM)
    vmem = pl.BlockSpec(memory_space=pltpu.VMEM)
    dma = pltpu.SemaphoreType.DMA
    cells = max(slots, rows_group * AGG)
    out = pl.pallas_call(
        functools.partial(kernel, n_row, n_col),
        out_shape=jax.ShapeDtypeStruct((KC * bw // 2, 2 * bw), BF16),
        in_specs=[keep] * 7,
        out_specs=vmem,
        scratch_shapes=[
            pltpu.VMEM((3, 1, slots), I32),
            pltpu.VMEM((1, 1), I32),
            pltpu.VMEM((1, dev_rows), I32),
            pltpu.VMEM((8, cells), I32),
            pltpu.SMEM((8, cells), I32),
            pltpu.VMEM((slots, 128), I32),
            pltpu.VMEM((slots, 128), I32),
            pltpu.VMEM((n_col, dev_rows, 128), I32),
            pltpu.VMEM((per, dev_rows, 128), I32),
            pltpu.VMEM((slots // 2, bw, 2 * bw), BF16),
            pltpu.VMEM((2, bw, 2 * bw), BF16),
            pltpu.VMEM((slots + 1, bw, 2 * bw), BF16),
            pltpu.VMEM((n_col, bw, dev_rows * bw), BF16),
            pltpu.VMEM((per, bw, dev_rows * bw), BF16),
            pltpu.VMEM((rows_group, bw, 2 * bw), BF16),
            pltpu.VMEM((cols_group, bw, bw), BF16),
            pltpu.VMEM((n_col, bw, bw), F32),
            pltpu.VMEM((n_col, bw // 2, 2 * bw), BF16),
            pltpu.VMEM((n_col, bw // 2, 2 * bw), BF16),
            dma((6,)), dma, dma,
            dma((2 * hi,)), dma((n_col,)),
            dma((n_col,)), dma((n_col,)),
            dma((per, n_row // 2)), dma((per,)),
            dma((n_row,)), dma,
            dma((n_col,)), dma((n_col,)),
        ],
        compiler_params=pltpu.CompilerParams(
            collective_id=0, has_side_effects=True, vmem_limit_bytes=67043328
        ),
    )(a_vals, p_vals, a_rows, a_cols, a_count, c_slot, agg.reshape(1, dev_rows))
    return out.astype(F32).reshape(1, KC * bw * bw)


def solution(mesh):
    return jax.shard_map(
        functools.partial(on_device, mesh.shape["row"], mesh.shape["col"]),
        mesh=mesh,
        in_specs=(
            P("row", "col"),
            P(None, ("row", "col")),
            P("row", "col"),
            P("row", "col"),
            P("row", "col"),
            P("row", "col"),
            P(("row", "col")),
        ),
        out_specs=P(("row", "col"), None),
        check_vma=False,
    )
```

time: 31.4 us -> 29.6 us (0.943)
  Pallas kernels: 29 us -> 27.3 us
    pallas_call x1, Pallas kernels: 29 us -> 27.3 us  [on_device(): pl.pallas_call(functools.partial(kernel, n_row, n_col), out_shape=jax.Sha...]
where the time goes in v1:
time: 29.6 us; the launch traced here: 29.4 us
  Pallas kernels  27.3 us (92%)
  other arithmetic  1.45 us (5%)
  between operations  0.66 us (2%)
    pallas_call x1, Pallas kernels, on_device(): pl.pallas_call(functools.partial(kernel, n_row, n_col), out_shape=jax.Sha...  27.3 us
    reshape x1, other arithmetic, on_device(): return out.astype(F32).reshape(1, KC * bw * bw)  1.45 us

profile of v1, /device:TPU:0, one launch (start us, length us, event | category | flops | bytes accessed | tf_op | source)
XLA Modules:
  0.0 29.4 jit_solution(5146283835228702093)
XLA Ops:
  0.7 27.3 %shard_map.73 = bf16[192,128]{1,0:T(8,128)(2,1)} custom-call(bf16[64,16384]{1,0:T(8,128)(2,1)} %a_hbm.1, bf16[64,512]{1,0:T(8,128)(2,1)} %p_hbm.1, s32[1,256]{1,0:T(1,128)} %rows_hbm.1, s32[1,256]{1,0:T(1,128)} %cols_hbm.1, s32[1,1]{1,0:T(1,128)S(6)} %copy.8.count_hbm, s32[1,256]{1,0:T(1,128)} %kslot_hbm.1, s32[1,8]{1,0:T(1,128)} %bitcast.2), custom_call_target="tpu_custom_call" | custom-call | tf_op jit(solution)/shard_map/pallas_call | solution.py:416
  27.9 1.4 %reshape.12 = f32[192,128]{1,0:T(8,128)} convert(bf16[192,128]{1,0:T(8,128)(2,1)} %shard_map.73) | non-fusion elementwise | flops 24576 | bytes 147456 | tf_op jit(solution)/shard_map/reshape | solution.py:452

commit v2 on v1

v2 whole, which is shorter than its diff:
```python
import functools
import math

import jax
import jax.numpy as jnp
from jax import lax
from jax.experimental import pallas as pl
from jax.experimental.pallas import tpu as pltpu
from jax.sharding import PartitionSpec as P

AGG = 8
KC = 6
LO = 2
MESH = pl.DeviceIdType.MESH
F32 = jnp.float32
BF16 = jnp.bfloat16
I32 = jnp.int32


def iota(shape, dim):
    return lax.broadcasted_iota(I32, shape, dim)


def within(at, size):
    return jnp.minimum(jnp.maximum(at, 0), size - 1)


def bits(n):
    return n.bit_length() - 1


def make_plan(rows_group, cols_group, ratio, small, count_v, plan_v):
    slots = small.shape[2]
    rb, cb, sb, ab = bits(rows_group), bits(cols_group), bits(slots), bits(AGG)
    groups = KC
    rows, cols = small[0], small[1]
    lane = iota((1, slots), 1)
    group = (rows >> cb) * (KC // ratio) + (small[2] >> bits(ratio))
    group = jnp.where(lane < count_v[...], group, groups)
    key = ((((group << rb) | rows) << cb | cols) << sb) | lane
    across = jnp.broadcast_to(key, (slots, slots))
    side, place = iota((slots, slots), 0), iota((slots, slots), 1)
    down = jnp.sum(jnp.where(side == place, across, 0), axis=1, keepdims=True)
    less = across < down
    rank = jnp.sum(jnp.where(less, 1, 0), axis=1, keepdims=True)
    cell_a, cell_d = key >> sb, down >> sb
    more = jnp.sum(jnp.where((cell_a == cell_d) & (across > down), 1, 0), axis=1, keepdims=True)
    word = jnp.sum(jnp.where(rank == place, down, 0), axis=0, keepdims=True)
    top = word >> sb
    same = (top == pltpu.roll(top, 1, 1)) & (lane > 0)
    word = (word & (slots - 1)) | (same.astype(I32) << 15)
    for g in range(slots // 128):
        plan_v[g:g + 1, :] = word[:, g * 128:(g + 1) * 128]

    def spots(line, n):
        line_a = (group << n) | line
        line_d = jnp.sum(jnp.where(side == place, line_a, 0), axis=1, keepdims=True)
        other = jnp.where((line_d == line_a) & (down < across), 1, 0)
        line_a = jnp.where(jnp.sum(other, axis=0, keepdims=True) == 0, line_a, -1)
        mine = (line_a < line_d) & (line_a >= (line_d >> n) << n)
        return line_d, jnp.sum(jnp.where(mine, 1, 0), axis=1, keepdims=True)

    line, down_at = spots(rows, rb)
    post, over_at = spots(cols, cb)
    group = line >> rb
    cell = (((group << ab) | down_at) << ab) | over_at
    tag = jnp.where((more == 0) & (group < groups), rank + 1, 0)
    at = slots // 128
    q = iota((slots, 128), 1)
    for g in range(groups * AGG * AGG // 128):
        found = jnp.sum(jnp.where(cell == q + g * 128, tag, 0), axis=0, keepdims=True)
        plan_v[at + g:at + g + 1, :] = jnp.where(found > 0, found - 1, slots)
    at += groups * AGG * AGG // 128
    line = jnp.where((group << ab) + down_at == q, line & (rows_group - 1), 0)
    post = jnp.where((group << ab) + over_at == q, post & (cols_group - 1), 0)
    line = jnp.max(line, axis=0, keepdims=True)
    post = jnp.max(post, axis=0, keepdims=True)
    plan_v[at:at + 1, :] = line | (post << 16)


def kernel(
    n_row, n_col, a_hbm, p_hbm, rows_hbm, cols_hbm, count_hbm, kslot_hbm, agg_hbm, out_ref,
    small, count_v, agg_v, plan_v, plan_s, from_v, from_s, agp, a_v, side, summed,
    pan, colp, flip, colb, mids, terms, packed, snd, rcv,
    in_sem, a_sem, plan_sem, from_sem, p_send, p_recv, g_send, g_recv, c_send, c_recv, x_send, x_recv,
):
    bw = p_hbm.shape[0]
    dev_rows = agg_v.shape[1]
    rows_group = n_col * dev_rows
    slots = small.shape[2]
    ratio = n_col // n_row
    per = n_col // ratio
    cols_group = per * dev_rows
    hi = n_col // LO
    half = bw // 2
    row = lax.axis_index("row")
    me = lax.axis_index("col")
    z, x = me // LO, lax.rem(me, LO)
    partner = z * LO + (1 - x)
    root = me // ratio
    part = lax.rem(me, ratio)
    is_root = row == root
    alike = lax.rem(row, 2) == lax.rem(root, 2)
    is_head = alike & jnp.logical_not(is_root)
    twin_row = row + 1 - 2 * lax.rem(row, 2)

    def col_of(d):
        return lax.rem(me + d, n_col)

    def row_of(d):
        return lax.rem(row + d, n_row)

    def z_of(d):
        return jnp.bitwise_xor(z, d)

    barrier = pltpu.get_barrier_semaphore()
    for d in range(1, n_col):
        pl.semaphore_signal(barrier, inc=1, device_id=(row, col_of(d)), device_id_type=MESH)
    for d in range(1, n_row):
        pl.semaphore_signal(barrier, inc=1, device_id=(row_of(d), me), device_id_type=MESH)
    loads = [
        pltpu.make_async_copy(src, dst, in_sem.at[i])
        for i, (src, dst) in enumerate(
            [
                (agg_hbm, agg_v),
                (rows_hbm, small.at[0]),
                (cols_hbm, small.at[1]),
                (count_hbm, count_v),
                (kslot_hbm, small.at[2]),
                (p_hbm, pan.at[me]),
            ]
        )
    ]
    for c in loads:
        c.start()
    pl.semaphore_wait(barrier, n_col + n_row - 2)

    def remote(src, dst, s, r, dev):
        return pltpu.make_async_remote_copy(
            src_ref=src, dst_ref=dst, send_sem=s, recv_sem=r, device_id=dev, device_id_type=MESH
        )

    def send_own(do):
        for d in range(1, hi):
            to = z_of(d) * LO + jnp.where(z_of(d) == row, me // per, x)
            do(remote(p_hbm, pan.at[me], p_send.at[d], p_recv.at[me], (row, to)))

    own = [remote(p_hbm, pan.at[me], p_send.at[3 * hi - 1], p_recv.at[me], (row, partner))]
    own[0].start()
    send_own(lambda c: c.start())

    def panel_copies(q, src):
        m = lax.rem(q, per)
        copies = [remote(src, colp.at[m], c_send.at[m, 0], c_recv.at[m], (twin_row, me))]
        for d in range(1, n_row // 2):
            copies.append(
                remote(src, colp.at[m], c_send.at[m, d], c_recv.at[m], (row_of(2 * d), me))
            )
        return copies

    def twin_copy(m):
        return remote(colp.at[m], colp.at[m], c_send.at[m, 0], c_recv.at[m], (twin_row, me))

    def panel_landed(m):
        remote(
            p_hbm, colp.at[m], c_send.at[m, 0], c_recv.at[m], (row, partner)
        ).wait_recv()

    def hand_on(q, src):
        @pl.when(is_root & (q // per == part))
        def _():
            for c in reversed(panel_copies(q, src)):
                c.start()

    hand_on(me, p_hbm)

    @pl.loop(0, slots // 16)
    def _(g):
        for u in range(8):
            i = g * 8 + u
            lanes = pl.ds(pl.multiple_of(i * (2 * bw), 2 * bw), 2 * bw)
            pltpu.make_async_copy(a_hbm.at[:, lanes], a_v.at[i], a_sem).start()

    loads[0].wait()
    square = (dev_rows, dev_rows)
    eye = iota(square, 0) == iota(square, 1)
    mine = jnp.where(eye, jnp.broadcast_to(agg_v[...], square), 0)
    mine = jnp.sum(mine, axis=1, keepdims=True)
    agp[me] = jnp.broadcast_to(mine, agp.shape[1:])
    marks = [
        remote(agp.at[me], agp.at[me], g_send.at[d - 1], g_recv.at[me], (row, col_of(d)))
        for d in range(1, n_col)
    ]
    for c in marks:
        c.start()
    for c in loads[1:]:
        c.wait()
    make_plan(rows_group, cols_group, ratio, small, count_v, plan_v)
    plan_copy = pltpu.make_async_copy(plan_v, plan_s, plan_sem)
    plan_copy.start()
    lanes = iota((bw, 2 * bw), 1)
    side[0] = (lanes < bw).astype(F32).astype(BF16)
    side[1] = (lanes >= bw).astype(F32).astype(BF16)
    summed[slots] = jnp.zeros((bw, 2 * bw), BF16)

    def landed(q):
        remote(p_hbm, pan.at[q], p_send.at[0], p_recv.at[q], (row, partner)).wait_recv()

    blank = jnp.zeros((bw, bw), BF16)

    def turn(q):
        for h in range(dev_rows // 2):
            t = pan[q, :, 2 * h * bw:2 * (h + 1) * bw].T
            for e in range(2):
                block, at = t[e * bw:(e + 1) * bw], q * dev_rows + 2 * h + e
                flip[2 * at] = jnp.concatenate([block, blank], axis=1)
                flip[2 * at + 1] = jnp.concatenate([blank, block], axis=1)

    pltpu.make_async_copy(a_v, a_v, a_sem).wait()

    plan_copy.wait()

    def sums(lo, hi_, acc):
        def body(i, acc):
            for u in range(8):
                word = plan_s[i >> 4, ((i & 15) << 3) + u]
                keep = ((word >> 15) & 1).astype(F32)
                pair = a_v[(word & (slots - 1)) >> 1] * side[word & 1]
                acc = acc * keep + pair.astype(F32)
                summed[8 * i + u] = acc.astype(BF16)
            return acc

        return lax.fori_loop(lo, hi_, body, acc)

    turn(me)
    acc = sums(0, slots // 16, jnp.zeros((bw, 2 * bw), F32))
    landed(partner)
    hand_on(partner, pan.at[partner])
    def pair(d):
        q = z_of(d) * LO + x
        return q, q + 1 - 2 * x, is_root & (q // per == x)

    def relay(q, at):
        return remote(pan.at[q], pan.at[q], p_send.at[at], p_recv.at[q], (row, partner))

    for d in range(1, hi):
        q, other, both = pair(d)

        @pl.when(both | jnp.logical_not(is_root))
        def _():
            landed(q)
            relay(q, hi - 1 + d).start()
            hand_on(q, pan.at[q])

        @pl.when(both)
        def _():
            landed(other)
            relay(other, 2 * hi - 1 + d).start()
            hand_on(other, pan.at[other])

    turn(partner)
    for d in range(1, hi):
        q, other, both = pair(d)

        @pl.when(both | jnp.logical_not(is_root))
        def _():
            turn(q)

        @pl.when(both)
        def _():
            turn(other)

    acc = sums(slots // 16, slots // 8, acc)
    for d in range(1, hi):
        q, other, both = pair(d)

        @pl.when(is_root & jnp.logical_not(both))
        def _():
            landed(q)
            turn(q)

        @pl.when(jnp.logical_not(both))
        def _():
            landed(other)
            turn(other)

    @pl.when(is_head)
    def _():
        for m in range(per):
            panel_landed(m)
            twin_copy(m).start()

    cells, lists = slots // 128, slots // 128 + KC * AGG * AGG // 128

    def listed(p, m):
        return plan_s[lists, p * AGG + m]

    for p in range(KC):
        left = jnp.concatenate(
            [
                flip[2 * (listed(p, 2 * h) & (rows_group - 1))]
                + flip[2 * (listed(p, 2 * h + 1) & (rows_group - 1)) + 1]
                for h in range(AGG // 2)
            ],
            axis=1,
        )

        def cell(m, n):
            at = (p * AGG + m) * AGG + n
            return summed[plan_s[cells + at // 128, at % 128]]

        mat = jnp.concatenate(
            [jnp.concatenate([cell(m, n) for n in range(AGG)], axis=1) for m in range(AGG)], axis=0
        )
        mids[p] = jnp.dot(left, mat, preferred_element_type=F32).astype(BF16)

    for d in range(1, n_col):
        q = col_of(d)
        remote(agp.at[q], agp.at[q], g_send.at[0], g_recv.at[q], (row, partner)).wait_recv()

    row_marks = jnp.concatenate([agp[c] for c in range(n_col)], axis=0)
    there = iota((rows_group, 2 * bw), 0) == small[0, 0:1, 0:1]
    first = jnp.sum(jnp.where(there, row_marks, 0), axis=0, keepdims=True)
    first = first * KC + small[2, 0:1, 0:1]
    owner = iota((1, 2 * bw), 1)
    slot = (first - KC * owner + 8 * n_col * n_col) & (n_col - 1)
    holds = (owner >> bits(per)) * (KC // ratio) + (slot >> bits(ratio))
    from_v[...] = jnp.where(slot < KC, holds, 0)
    from_copy = pltpu.make_async_copy(from_v, from_s, from_sem)
    from_copy.start()
    def unpack(m, src):
        for b in range(dev_rows):
            colb[m * dev_rows + b] = src[:, b * bw:(b + 1) * bw]

    for m in range(per):
        @pl.when(is_root)
        def _():
            unpack(m, pan.at[part * per + m])

        @pl.when(jnp.logical_not(is_root))
        def _():
            @pl.when(jnp.logical_not(is_head))
            def _():
                panel_landed(m)

            unpack(m, colp.at[m])

    for p in range(KC):
        right = jnp.concatenate(
            [colb[(listed(p, n // 2) >> 16) & (cols_group - 1)] for n in range(2 * AGG)], axis=0
        )
        terms[p] = jnp.dot(mids[p], right, preferred_element_type=F32)
    for p in range(KC):
        even = terms[p, pl.ds(0, half, stride=2), :]
        odd = terms[p, pl.ds(1, half, stride=2), :]
        packed[p] = jnp.concatenate([even, odd], axis=1).astype(BF16)
    from_copy.wait()
    for o in range(n_col):
        snd[o] = packed[within(from_s[0, o], KC)]

    def term(o):
        return remote(snd.at[o], rcv.at[me], x_send.at[o], x_recv.at[me], (row, o))

    for o in range(n_col):
        @pl.when(me != o)
        def _():
            term(o).start()

    rcv[me] = snd[me]
    for d in range(1, n_col):
        q = col_of(d)
        remote(snd.at[0], rcv.at[q], x_send.at[0], x_recv.at[q], (row, partner)).wait_recv()
    total = [jnp.zeros((half, 2 * bw), F32) for _ in range(KC)]
    for c in range(n_col):
        value = rcv[c].astype(F32)
        where = (first + (c - (KC + 1) * me + 8 * n_col * n_col)) & (n_col - 1)
        for k in range(KC):
            total[k] += jnp.where(where == k, value, 0.0)
    for k in range(KC):
        out_ref[k * half:(k + 1) * half, :] = total[k].astype(BF16)

    for c in own + marks:
        c.wait_send()
    for d in range(1, hi):
        q, other, both = pair(d)

        @pl.when(both | jnp.logical_not(is_root))
        def _():
            relay(q, hi - 1 + d).wait_send()

        @pl.when(both)
        def _():
            relay(other, 2 * hi - 1 + d).wait_send()

    send_own(lambda c: c.wait_send())
    for o in range(n_col):
        @pl.when(me != o)
        def _():
            term(o).wait_send()

    @pl.when(is_root)
    def _():
        for m in range(per):
            for c in panel_copies(m, pan.at[0]):
                c.wait_send()

    @pl.when(is_head)
    def _():
        for m in range(per):
            twin_copy(m).wait_send()


def on_device(n_row, n_col, a_vals, p_vals, a_rows, a_cols, a_count, c_slot, agg):
    bw = p_vals.shape[0]
    dev_rows = agg.shape[0]
    slots = a_rows.shape[1]
    rows_group = dev_rows * n_col
    ratio = n_col // n_row
    per = n_col // ratio
    cols_group = per * dev_rows
    hi = n_col // LO
    assert rows_group // AGG == n_col and n_col >= KC and n_row % 2 == 0
    assert ratio == LO and hi == n_row
    assert math.gcd(KC, n_col) == ratio and slots % 128 == 0 and 2 * bw == 128
    assert all(n & (n - 1) == 0 for n in (n_col, slots, cols_group, dev_rows, hi))
    keep = pl.BlockSpec(memory_space=pltpu.HBM)
    vmem = pl.BlockSpec(memory_space=pltpu.VMEM)
    dma = pltpu.SemaphoreType.DMA
    out = pl.pallas_call(
        functools.partial(kernel, n_row, n_col),
        out_shape=jax.ShapeDtypeStruct((KC * bw // 2, 2 * bw), BF16),
        in_specs=[keep] * 7,
        out_specs=vmem,
        scratch_shapes=[
            pltpu.VMEM((3, 1, slots), I32),
            pltpu.VMEM((1, 1), I32),
            pltpu.VMEM((1, dev_rows), I32),
            pltpu.VMEM((8, 128), I32),
            pltpu.SMEM((8, 128), I32),
            pltpu.VMEM((1, 128), I32),
            pltpu.SMEM((1, 128), I32),
            pltpu.VMEM((n_col, dev_rows, 128), I32),
            pltpu.VMEM((slots // 2, bw, 2 * bw), BF16),
            pltpu.VMEM((2, bw, 2 * bw), BF16),
            pltpu.VMEM((slots + 1, bw, 2 * bw), BF16),
            pltpu.VMEM((n_col, bw, dev_rows * bw), BF16),
            pltpu.VMEM((per, bw, dev_rows * bw), BF16),
            pltpu.VMEM((2 * rows_group, bw, 2 * bw), BF16),
            pltpu.VMEM((cols_group, bw, bw), BF16),
            pltpu.VMEM((KC, bw, 2 * AGG * bw), BF16),
            pltpu.VMEM((KC, bw, bw), F32),
            pltpu.VMEM((KC, bw // 2, 2 * bw), BF16),
            pltpu.VMEM((n_col, bw // 2, 2 * bw), BF16),
            pltpu.VMEM((n_col, bw // 2, 2 * bw), BF16),
            dma((6,)), dma, dma, dma,
            dma((3 * hi,)), dma((n_col,)),
            dma((n_col,)), dma((n_col,)),
            dma((per, n_row // 2)), dma((per,)),
            dma((n_col,)), dma((n_col,)),
        ],
        compiler_params=pltpu.CompilerParams(
            collective_id=0, has_side_effects=True, vmem_limit_bytes=67043328
        ),
    )(a_vals, p_vals, a_rows, a_cols, a_count, c_slot, agg.reshape(1, dev_rows))
    return out.astype(F32).reshape(1, KC * bw * bw)


def solution(mesh):
    return jax.shard_map(
        functools.partial(on_device, mesh.shape["row"], mesh.shape["col"]),
        mesh=mesh,
        in_specs=(
            P("row", "col"),
            P(None, ("row", "col")),
            P("row", "col"),
            P("row", "col"),
            P("row", "col"),
            P("row", "col"),
            P(("row", "col")),
        ),
        out_specs=P(("row", "col"), None),
        check_vma=False,
    )
```

time: 29.6 us -> 27 us (0.912)
  Pallas kernels: 27.3 us -> 24.7 us
    pallas_call x1, Pallas kernels: 27.3 us -> 24.7 us  [on_device(): pl.pallas_call(functools.partial(kernel, n_row, n_col), out_shape=jax.Sha...]
where the time goes in v2:
time: 27 us; the launch traced here: 26.8 us
  Pallas kernels  24.7 us (91%)
  other arithmetic  1.45 us (5%)
  between operations  0.66 us (2%)
    pallas_call x1, Pallas kernels, on_device(): pl.pallas_call(functools.partial(kernel, n_row, n_col), out_shape=jax.Sha...  24.7 us
    reshape x1, other arithmetic, on_device(): return out.astype(F32).reshape(1, KC * bw * bw)  1.45 us

profile of v2, /device:TPU:0, one launch (start us, length us, event | category | flops | bytes accessed | tf_op | source)
XLA Modules:
  0.0 26.8 jit_solution(6493224018779085681)
XLA Ops:
  0.7 24.7 %shard_map.73 = bf16[192,128]{1,0:T(8,128)(2,1)} custom-call(bf16[64,16384]{1,0:T(8,128)(2,1)} %a_hbm.1, bf16[64,512]{1,0:T(8,128)(2,1)} %p_hbm.1, s32[1,256]{1,0:T(1,128)} %rows_hbm.1, s32[1,256]{1,0:T(1,128)} %cols_hbm.1, s32[1,1]{1,0:T(1,128)S(6)} %copy.8.count_hbm, s32[1,256]{1,0:T(1,128)} %kslot_hbm.1, s32[1,8]{1,0:T(1,128)} %bitcast.2), custom_call_target="tpu_custom_call" | custom-call | tf_op jit(solution)/shard_map/pallas_call | solution.py:429
  25.3 1.4 %reshape.12 = f32[192,128]{1,0:T(8,128)} convert(bf16[192,128]{1,0:T(8,128)(2,1)} %shard_map.73) | non-fusion elementwise | flops 24576 | bytes 147456 | tf_op jit(solution)/shard_map/reshape | solution.py:465

commit v3 on v2

--- a/solution.py
+++ b/solution.py
@@ -141,9 +141,17 @@
         )
 
     def send_own(do):
+        def to(at, target, side):
+            do(remote(p_hbm, pan.at[me], p_send.at[at], p_recv.at[me], (row, target * LO + side)))
+
+        @pl.when(row != z)
+        def _():
+            to(0, row, me // per)
+
         for d in range(1, hi):
-            to = z_of(d) * LO + jnp.where(z_of(d) == row, me // per, x)
-            do(remote(p_hbm, pan.at[me], p_send.at[d], p_recv.at[me], (row, to)))
+            @pl.when(z_of(d) != row)
+            def _():
+                to(d, z_of(d), x)
 
     own = [remote(p_hbm, pan.at[me], p_send.at[3 * hi - 1], p_recv.at[me], (row, partner))]
     own[0].start()
@@ -258,6 +266,15 @@
             relay(other, 2 * hi - 1 + d).start()
             hand_on(other, pan.at[other])
 
+    def unpack(m, src):
+        for b in range(dev_rows):
+            colb[m * dev_rows + b] = src[:, b * bw:(b + 1) * bw]
+
+    @pl.when(is_root)
+    def _():
+        for m in range(per):
+            unpack(m, pan.at[part * per + m])
+
     turn(partner)
     for d in range(1, hi):
         q, other, both = pair(d)
@@ -271,7 +288,59 @@
             turn(other)
 
     acc = sums(slots // 16, slots // 8, acc)
-    for d in range(1, hi):
+    cells, lists = slots // 128, slots // 128 + KC * AGG * AGG // 128
+
+    def listed(p, m):
+        return plan_s[lists, p * AGG + m]
+
+    part_groups = KC // ratio
+
+    def mid(h):
+        for g in range(part_groups):
+            p = h * part_groups + g
+            left = jnp.concatenate(
+                [
+                    flip[2 * (listed(p, 2 * h) & (rows_group - 1))]
+                    + flip[2 * (listed(p, 2 * h + 1) & (rows_group - 1)) + 1]
+                    for h in range(AGG // 2)
+                ],
+                axis=1,
+            )
+
+            def cell(m, n):
+                at = (p * AGG + m) * AGG + n
+                return summed[plan_s[cells + (at >> 7), at & 127]]
+
+            mat = jnp.concatenate(
+                [jnp.concatenate([cell(m, n) for n in range(AGG)], axis=1) for m in range(AGG)], axis=0
+            )
+            mids[p] = jnp.dot(left, mat, preferred_element_type=F32).astype(BF16)
+
+    near = z // (hi // ratio)
+
+    for d in range(1, hi // ratio):
+        q, other, both = pair(d)
+
+        @pl.when(is_root & jnp.logical_not(both))
+        def _():
+            landed(q)
+            turn(q)
+
+        @pl.when(jnp.logical_not(both))
+        def _():
+            landed(other)
+            turn(other)
+
+    is_mate = twin_row == root
+
+    @pl.when(is_mate)
+    def _():
+        for m in range(per):
+            panel_landed(m)
+            unpack(m, colp.at[m])
+
+    mid(near)
+    for d in range(hi // ratio, hi):
         q, other, both = pair(d)
 
         @pl.when(is_root & jnp.logical_not(both))
@@ -290,30 +359,8 @@
             panel_landed(m)
             twin_copy(m).start()
 
-    cells, lists = slots // 128, slots // 128 + KC * AGG * AGG // 128
-
-    def listed(p, m):
-        return plan_s[lists, p * AGG + m]
-
-    for p in range(KC):
-        left = jnp.concatenate(
-            [
-                flip[2 * (listed(p, 2 * h) & (rows_group - 1))]
-                + flip[2 * (listed(p, 2 * h + 1) & (rows_group - 1)) + 1]
-                for h in range(AGG // 2)
-            ],
-            axis=1,
-        )
-
-        def cell(m, n):
-            at = (p * AGG + m) * AGG + n
-            return summed[plan_s[cells + at // 128, at % 128]]
-
-        mat = jnp.concatenate(
-            [jnp.concatenate([cell(m, n) for n in range(AGG)], axis=1) for m in range(AGG)], axis=0
-        )
-        mids[p] = jnp.dot(left, mat, preferred_element_type=F32).astype(BF16)
-
+    for h in range(1, ratio):
+        mid(lax.rem(near + h, ratio))
     for d in range(1, n_col):
         q = col_of(d)
         remote(agp.at[q], agp.at[q], g_send.at[0], g_recv.at[q], (row, partner)).wait_recv()
@@ -328,16 +375,8 @@
     from_v[...] = jnp.where(slot < KC, holds, 0)
     from_copy = pltpu.make_async_copy(from_v, from_s, from_sem)
     from_copy.start()
-    def unpack(m, src):
-        for b in range(dev_rows):
-            colb[m * dev_rows + b] = src[:, b * bw:(b + 1) * bw]
-
     for m in range(per):
-        @pl.when(is_root)
-        def _():
-            unpack(m, pan.at[part * per + m])
-
-        @pl.when(jnp.logical_not(is_root))
+        @pl.when(jnp.logical_not(is_root | is_mate))
         def _():
             @pl.when(jnp.logical_not(is_head))
             def _():
@@ -408,6 +447,10 @@
     def _():
         for m in range(per):
             twin_copy(m).wait_send()
+
+
+def hbm(value):
+    return pltpu.with_memory_space_constraint(value, pltpu.HBM)
 
 
 def on_device(n_row, n_col, a_vals, p_vals, a_rows, a_cols, a_count, c_slot, agg):
@@ -459,9 +502,12 @@
             dma((n_col,)), dma((n_col,)),
         ],
         compiler_params=pltpu.CompilerParams(
-            collective_id=0, has_side_effects=True, vmem_limit_bytes=67043328
+            collective_id=0, has_side_effects=True, vmem_limit_bytes=40 * 1024 * 1024
         ),
-    )(a_vals, p_vals, a_rows, a_cols, a_count, c_slot, agg.reshape(1, dev_rows))
+    )(
+        hbm(a_vals), hbm(p_vals), hbm(a_rows), hbm(a_cols), a_count, hbm(c_slot),
+        hbm(agg.reshape(1, dev_rows)),
+    )
     return out.astype(F32).reshape(1, KC * bw * bw)
 
 

time: 27 us -> 24.8 us (0.919)
  Pallas kernels: 24.7 us -> 23.3 us
  other arithmetic: 1.45 us -> 0.65 us
    pallas_call x1, Pallas kernels: 24.7 us -> 23.3 us  [on_device(): pl.pallas_call(functools.partial(kernel, n_row, n_col), out_shape=jax.Sha...]
    reshape x1, other arithmetic: 1.45 us -> 0.65 us  [on_device(): return out.astype(F32).reshape(1, KC * bw * bw)]
where the time goes in v3:
time: 24.8 us; the launch traced here: 24.6 us
  Pallas kernels  23.3 us (94%)
  between operations  0.66 us (3%)
  other arithmetic  0.65 us (3%)
    pallas_call x1, Pallas kernels, on_device(): pl.pallas_call(functools.partial(kernel, n_row, n_col), out_shape=jax.Sha...  23.3 us
    reshape x1, other arithmetic, on_device(): return out.astype(F32).reshape(1, KC * bw * bw)  0.65 us

profile of v3, /device:TPU:0, one launch (start us, length us, event | category | flops | bytes accessed | tf_op | source)
XLA Modules:
  0.0 24.6 jit_solution(3143259886477111068)
XLA Ops:
  0.7 23.3 %shard_map.73 = bf16[192,128]{1,0:T(8,128)(2,1)S(1)} custom-call(bf16[64,16384]{1,0:T(8,128)(2,1)} %a_hbm.1, bf16[64,512]{1,0:T(8,128)(2,1)} %p_hbm.1, s32[1,256]{1,0:T(1,128)} %rows_hbm.1, s32[1,256]{1,0:T(1,128)} %cols_hbm.1, s32[1,1]{1,0:T(1,128)S(6)} %copy.8.count_hbm, s32[1,256]{1,0:T(1,128)} %kslot_hbm.1, s32[1,8]{1,0:T(1,128)} %bitcast.2), custom_call_target="tpu_custom_call" | custom-call | tf_op jit(solution)/shard_map/pallas_call | solution.py:472
  24.0 0.6 %reshape.12 = f32[192,128]{1,0:T(8,128)} convert(bf16[192,128]{1,0:T(8,128)(2,1)S(1)} %shard_map.73) | non-fusion elementwise | flops 24576 | bytes 147456 | tf_op jit(solution)/shard_map/reshape | solution.py:511

commit v4 on v3

--- a/solution.py
+++ b/solution.py
@@ -266,6 +266,10 @@
             relay(other, 2 * hi - 1 + d).start()
             hand_on(other, pan.at[other])
 
+        if d == 1:
+            turn(partner)
+            acc = sums(slots // 16, slots // 8, acc)
+
     def unpack(m, src):
         for b in range(dev_rows):
             colb[m * dev_rows + b] = src[:, b * bw:(b + 1) * bw]
@@ -275,7 +279,6 @@
         for m in range(per):
             unpack(m, pan.at[part * per + m])
 
-    turn(partner)
     for d in range(1, hi):
         q, other, both = pair(d)
 
@@ -287,7 +290,6 @@
         def _():
             turn(other)
 
-    acc = sums(slots // 16, slots // 8, acc)
     cells, lists = slots // 128, slots // 128 + KC * AGG * AGG // 128
 
     def listed(p, m):
@@ -298,6 +300,8 @@
     def mid(h):
         for g in range(part_groups):
             p = h * part_groups + g
+            fold = 128 // (AGG * AGG)
+            line, lane = cells + p // fold, p % fold * (AGG * AGG)
             left = jnp.concatenate(
                 [
                     flip[2 * (listed(p, 2 * h) & (rows_group - 1))]
@@ -308,8 +312,7 @@
             )
 
             def cell(m, n):
-                at = (p * AGG + m) * AGG + n
-                return summed[plan_s[cells + (at >> 7), at & 127]]
+                return summed[plan_s[line, lane + m * AGG + n]]
 
             mat = jnp.concatenate(
                 [jnp.concatenate([cell(m, n) for n in range(AGG)], axis=1) for m in range(AGG)], axis=0
@@ -339,28 +342,8 @@
             panel_landed(m)
             unpack(m, colp.at[m])
 
-    mid(near)
-    for d in range(hi // ratio, hi):
-        q, other, both = pair(d)
-
-        @pl.when(is_root & jnp.logical_not(both))
-        def _():
-            landed(q)
-            turn(q)
-
-        @pl.when(jnp.logical_not(both))
-        def _():
-            landed(other)
-            turn(other)
-
-    @pl.when(is_head)
-    def _():
-        for m in range(per):
-            panel_landed(m)
-            twin_copy(m).start()
-
-    for h in range(1, ratio):
-        mid(lax.rem(near + h, ratio))
+    for h in range(ratio):
+        pl.when(near == h)(functools.partial(mid, h))
     for d in range(1, n_col):
         q = col_of(d)
         remote(agp.at[q], agp.at[q], g_send.at[0], g_recv.at[q], (row, partner)).wait_recv()
@@ -375,6 +358,27 @@
     from_v[...] = jnp.where(slot < KC, holds, 0)
     from_copy = pltpu.make_async_copy(from_v, from_s, from_sem)
     from_copy.start()
+    for d in range(hi // ratio, hi):
+        q, other, both = pair(d)
+
+        @pl.when(is_root & jnp.logical_not(both))
+        def _():
+            landed(q)
+            turn(q)
+
+        @pl.when(jnp.logical_not(both))
+        def _():
+            landed(other)
+            turn(other)
+
+    @pl.when(is_head)
+    def _():
+        for m in range(per):
+            panel_landed(m)
+            twin_copy(m).start()
+
+    for h in range(ratio):
+        pl.when(near != h)(functools.partial(mid, h))
     for m in range(per):
         @pl.when(jnp.logical_not(is_root | is_mate))
         def _():

time: 24.8 us -> 24.5 us (0.988)
  Pallas kernels: 23.3 us -> 23 us
    pallas_call x1, Pallas kernels: 23.3 us -> 23 us  [on_device(): pl.pallas_call(functools.partial(kernel, n_row, n_col), out_shape=jax.Sha...]
where the time goes in v4:
time: 24.5 us; the launch traced here: 24.3 us
  Pallas kernels  23 us (94%)
  between operations  0.66 us (3%)
  other arithmetic  0.65 us (3%)
    pallas_call x1, Pallas kernels, on_device(): pl.pallas_call(functools.partial(kernel, n_row, n_col), out_shape=jax.Sha...  23 us
    reshape x1, other arithmetic, on_device(): return out.astype(F32).reshape(1, KC * bw * bw)  0.65 us

profile of v4, /device:TPU:0, one launch (start us, length us, event | category | flops | bytes accessed | tf_op | source)
XLA Modules:
  0.0 24.3 jit_solution(14537602643383799808)
XLA Ops:
  0.7 23.0 %shard_map.73 = bf16[192,128]{1,0:T(8,128)(2,1)S(1)} custom-call(bf16[64,16384]{1,0:T(8,128)(2,1)} %a_hbm.1, bf16[64,512]{1,0:T(8,128)(2,1)} %p_hbm.1, s32[1,256]{1,0:T(1,128)} %rows_hbm.1, s32[1,256]{1,0:T(1,128)} %cols_hbm.1, s32[1,1]{1,0:T(1,128)S(6)} %copy.8.count_hbm, s32[1,256]{1,0:T(1,128)} %kslot_hbm.1, s32[1,8]{1,0:T(1,128)} %bitcast.2), custom_call_target="tpu_custom_call" | custom-call | tf_op jit(solution)/shard_map/pallas_call | solution.py:476
  23.7 0.6 %reshape.12 = f32[192,128]{1,0:T(8,128)} convert(bf16[192,128]{1,0:T(8,128)(2,1)S(1)} %shard_map.73) | non-fusion elementwise | flops 24576 | bytes 147456 | tf_op jit(solution)/shard_map/reshape | solution.py:515
